TPU v7x, 32 devices: a whole 2x2x4 slice. The times are simulated.
32 devices in a mesh: tm: 2 (over y), pts: 16 (over z, x, core).
Axes of the slice: x: 2, y: 2, z: 4, core: 2. Of those that a mesh axis runs over, the one named last changes fastest.
Arguments:
- precip: float32 [512, 16384], P('tm', 'pts'), may hold values from -150 to 300, as said below
- thresholds: float32 [64], replicated, may hold values from -1 to 5
- bin_index: int32 [16384], P('pts'), may hold values from 0 to 63
- test_matrix: float32 [512, 256], P('tm'), may hold values from -0.25 to 0.25
Outputs:
- basis: float32 [16384, 256], P(('pts', 'tm'))
- factor: float32 [256, 256], replicated
Inputs may be any that keep to these rules, and one draw needn't show every extreme that they name: `precip`: precipitation records.
All inputs are finite; a program needn't handle non-finite values.
Results may differ from a plain program's by a relative error of at most 0.0003.
Values sent between devices are 32-bit elements; how exact they have to be, the bound alone decides.
No kernel may reach another device: no remote copies, remote signals or barrier semaphores. Data moves between devices by JAX's collectives and lax.ppermute only.
A program may use at most 64 MiB of HBM per device.

v0:
```python
import math

import jax
import jax.numpy as jnp
from jax import lax
from jax.sharding import PartitionSpec as P

HARM = 8


year_days = 365.25


def harmonic_table(day_number):
    phase_base = day_number.astype(jnp.float32)
    columns = [jnp.ones_like(phase_base)]
    for order in range(1, HARM + 1):
        phase = 2.0 * math.pi * order / year_days * phase_base
        columns.append(jnp.cos(phase))
        columns.append(jnp.sin(phase))
    return jnp.stack(columns, 0)


def normal_solve(factor_low, values):
    forward = lax.linalg.triangular_solve(factor_low, values, left_side=True, lower=True)
    return lax.linalg.triangular_solve(
        factor_low, forward, left_side=True, lower=True, transpose_a=True
    )


def on_device(precip, thresholds, bin_index, test_matrix):
    highest = lax.Precision.HIGHEST
    tm_count = lax.axis_size("tm")
    tm_place = lax.axis_index("tm")
    days_local, points_local = precip.shape
    own_rows = points_local // tm_count
    days_total = days_local * tm_count
    points_total = points_local * lax.axis_size("pts")
    full_table = harmonic_table(jnp.arange(days_total, dtype=jnp.int32))
    normal = jnp.dot(full_table, full_table.T, precision=highest)
    normal_low = jnp.linalg.cholesky(normal)
    one_hot = (
        bin_index[:, None] == jnp.arange(thresholds.shape[0], dtype=jnp.int32)[None, :]
    ).astype(jnp.float32)
    level_local = jnp.dot(one_hot, thresholds, precision=highest)
    series = lax.all_to_all(precip, "tm", split_axis=1, concat_axis=0, tiled=True)
    projections = jnp.dot(full_table, series, precision=highest)
    coefficients = normal_solve(normal_low, projections)
    anomaly = series - lax.dot_general(
        full_table, coefficients, (((0,), (0,)), ((), ())), precision=highest
    )
    level_own = lax.dynamic_slice_in_dim(level_local, tm_place * own_rows, own_rows, 0)
    excess = jnp.maximum(anomaly - level_own[None, :], 0.0)
    sketch = lax.dot_general(
        excess,
        lax.all_gather(test_matrix, "tm", axis=0, tiled=True),
        (((0,), (0,)), ((), ())),
        precision=highest,
    )
    local_cross = jnp.dot(sketch.T, sketch, precision=highest)
    cross = lax.psum(local_cross, ("tm", "pts")) / points_total
    lower = jnp.linalg.cholesky(cross)
    basis = lax.linalg.triangular_solve(
        lower, sketch, left_side=False, lower=True, transpose_a=True
    )
    return (basis, lower.T)


def solution(mesh):
    in_specs = (P("tm", "pts"), P(), P("pts"), P("tm", None))
    out_specs = (P(("pts", "tm"), None), P())
    return jax.shard_map(
        on_device, mesh=mesh, in_specs=in_specs, out_specs=out_specs, check_vma=False
    )
```

profile of v0, /device:TPU:0, one launch (start us, length us, event | category | flops | bytes accessed | tf_op | source)
XLA Modules:
  0.0 239.9 jit_solution(151745460455063084)
XLA Ops:
  7.2 2.5 %copy.16 = f32[256,1024]{0,1:T(8,128)} copy(f32[256,1024]{1,0:T(8,128)} %param.4) | data formatting | bytes 2097152 | tf_op args[0]
  9.7 4.3 %all-to-all-start = ((f32[256,2,512]{0,2,1:T(8,128)}), f32[256,2,512]{0,2,1:T(8,128)S(1)}, u32[]{:S(2)}, u32[]{:S(2)}) async-start(f32[256,2,512]{0,2,1:T(8,128)} %bitcast), calls=%async_computation | async-start | bytes 2097152 | tf_op jit(solution)/shard_map/all_to_all | solution.py:46
  14.1 0.1 fusion.22
  14.2 0.1 fusion.24
  14.2 0.1 fusion.26
  14.3 0.1 fusion.28
  14.4 0.1 fusion.30
  14.5 0.1 fusion.32
  14.7 0.1 stack.2
  14.8 0.2 fusion.38
  14.9 0.1 copy.18
  15.0 1.5 cholesky.60
  16.6 0.6 compare_reduce_fusion.2
  17.3 0.6 fusion.14
  17.9 1.3 custom-call.22
  19.2 0.7 copy-done.3
  19.9 0.4 fusion.2
  20.4 0.1 dynamic_slice.3
  20.5 13.6 %all_gather.3 = f32[512,256]{1,0:T(8,128)S(1)} all-gather(f32[256,256]{1,0:T(8,128)S(1)} %copy-done.2), channel_id=1, replica_groups=mesh['tm'=2,'pts'=16] {'tm'}, dimensions={0}, use_global_device_ids=true | all-gather | bytes 786432 | tf_op jit(solution)/shard_map/all_gather | solution.py:56
  34.0 0.3 copy.17
  34.4 0.6 fusion.39
  35.0 0.2 fusion.17
  35.2 0.2 fusion.15
  35.4 1.1 fusion.1
  36.5 1.9 fusion.40
  38.4 1.7 fusion.41
  40.2 127.2 %all-reduce.3.cloned.1.call-done = f32[256,256]{0,1:T(8,128)} async-done(((f32[256,256]{0,1:T(8,128)}), f32[256,256]{0,1:T(8,128)}) %all-reduce.3.cloned.1.call-update) | async-done | bytes 262160 | tf_op jit(solution)/shard_map/psum | solution.py:61
  167.4 1.0 broadcast_multiply_fusion
  168.4 0.1 copy.20
  168.5 0.8 copy-done.1
  169.4 11.7 %cholesky.123 = f32[128,128]{1,0:T(8,128)S(1)} custom-call(f32[128,128]{1,0:T(8,128)S(1)} %cholesky.153), custom_call_target="Cholesky" | custom-call | tf_op jit(solution)/shard_map/jit(cholesky)/cholesky | solution.py:62
  181.1 9.8 %custom-call.23 = f32[1,128,128]{1,2,0:T(8,128)S(1)} custom-call(f32[1,128,128]{2,1,0:T(8,128)S(1)} %get-tuple-element.31), custom_call_target="InvertDiagBlocksLowerTriangular" | custom-call | tf_op jit(solution)/shard_map/jit(cholesky)/cholesky | solution.py:62
  190.9 0.2 constant_dynamic-update-slice_fusion.1
  191.2 0.3 convolution_subtract_fusion.2
  191.4 11.9 %cholesky.140 = f32[128,128]{1,0:T(8,128)S(1)} custom-call(f32[128,128]{1,0:T(8,128)S(1)} %convolution_subtract_fusion.2), custom_call_target="Cholesky" | custom-call | tf_op jit(solution)/shard_map/jit(cholesky)/cholesky | solution.py:62
  203.3 0.7 compare_reduce_fusion
  204.1 0.6 compare_reduce_fusion.1
  206.1 4.0 %while.1 = (s32[]{:T(128)}, f32[256,256]{1,0:T(8,128)S(1)}, s32[2,2]{1,0:T(2,128)S(1)}, f32[2,128,128]{2,1,0:T(8,128)S(1)}, s32[]{:T(128)}) while((s32[]{:T(128)}, f32[256,256]{1,0:T(8,128)S(1)}, s32[2,2]{1,0:T(2,128)S(1)}, f32[2,128,128]{2,1,0:T(8,128)S(1)}, s32[]{:T(128)}) %tuple.38), condition=%wide.while_cond, body=%wide.while_body.sunk | while | flops 2 | bytes 131181 | solution.py:63
  206.1 0.6 fusion.59
  206.7 1.4 bitcast_dynamic-update-slice_fusion.2
  208.1 0.6 fusion.59
  208.7 1.4 bitcast_dynamic-update-slice_fusion.2
  210.1 19.7 %custom-call.24 = f32[2,128,128]{1,2,0:T(8,128)S(1)} custom-call(f32[2,128,128]{2,1,0:T(8,128)S(1)} %get-tuple-element.9), custom_call_target="InvertDiagBlocksLowerTriangular" | custom-call | tf_op jit(solution)/shard_map/triangular_solve | solution.py:63
  229.7 0.4 fusion.3
  230.2 0.6 convolution_subtract_fusion.1
  230.8 0.4 fusion.9
  231.2 1.0 copy.21
  232.2 0.8 copy.22
  (26 shorter events, 0.5 us)
Async XLA Ops:
  7.2 12.1 %copy-start = (f32[64]{0:T(128)S(1)}, f32[64]{0:T(128)}, u32[]{:S(2)}) copy-start(f32[64]{0:T(128)} %param.5) | copy-start | bytes 772
  9.7 24.3 %all-to-all-start = ((f32[256,2,512]{0,2,1:T(8,128)}), f32[256,2,512]{0,2,1:T(8,128)S(1)}, u32[]{:S(2)}, u32[]{:S(2)}) async-start(f32[256,2,512]{0,2,1:T(8,128)} %bitcast), calls=%async_computation | async-start | bytes 2097152 | tf_op jit(solution)/shard_map/all_to_all | solution.py:46
  14.0 153.4 %all-reduce.3.cloned.1.call-start = ((), (), s32[]{:S(2)}) async-start(), calls=%async_computation.1 | async-start | bytes 524288 | tf_op jit(solution)/shard_map/psum | solution.py:61
  14.1 6.4 %copy-start.2 = (f32[256,256]{1,0:T(8,128)S(1)}, f32[256,256]{1,0:T(8,128)}, u32[]{:S(2)}) copy-start(f32[256,256]{1,0:T(8,128)} %param.7) | copy-start | bytes 786436
  19.2 0.7 copy-start.3
  168.4 1.0 copy-start.1
Sparse Core Ops, SparseCore 0:
  40.3 127.0 all-reduce.2
where the time goes:
time: 240 us
  waiting for transfers between devices  127 us (53%)
  other arithmetic  60.4 us (25%)
  between operations  15.6 us (6%)
  blocking collectives  13.6 us (6%)
  local copies, waits for them, and re-layouts  10.7 us (4%)
  matrix products  8.22 us (3%)
  starting transfers between devices  4.26 us (2%)
    psum x1, waiting for transfers between devices, on_device(): cross = lax.psum(local_cross, ('tm', 'pts')) / points_total  127 us
    another operation x7, other arithmetic, on_device(): lower = jnp.linalg.cholesky(cross)  34.8 us
    another operation x3, other arithmetic, on_device(): lax.linalg.triangular_solve(lower, sketch, left_side=False, lower=True, t...  19.7 us
    all_gather x1, blocking collectives, on_device(): lax.all_gather(test_matrix, 'tm', axis=0, tiled=True)  13.6 us
    unnamed x11, local copies, waits for them, and re-layouts  5.9 us
  transfers between devices with their start and end apart: 2, of which 1 were waited for; matrix products, arithmetic and copies ran while one was open for 2% of the time, Pallas kernels for 0%

commit v1 on v0

--- a/solution.py
+++ b/solution.py
@@ -28,6 +28,40 @@
     )
 
 
+AXES = ("tm", "pts")
+
+
+def swap(value, bit):
+    total = lax.axis_size("tm") * lax.axis_size("pts")
+    return lax.ppermute(value, AXES, [(i, i ^ bit) for i in range(total)])
+
+
+def all_days(block, count, place, stride):
+    pieces = [block] + [swap(block, step * stride) for step in range(1, count)]
+    stack = jnp.stack(pieces)
+    order = place ^ jnp.arange(count)
+    return stack[order].reshape((-1,) + block.shape[1:])
+
+
+def sum_all(value):
+    total = lax.axis_size("tm") * lax.axis_size("pts")
+    low = lax.axis_index("pts") % 2
+    half = value.shape[0] // 2
+    kept = lax.dynamic_slice_in_dim(value, low * half, half, 0)
+    sent = lax.dynamic_slice_in_dim(value, (1 - low) * half, half, 0)
+    part = kept + swap(sent, 1)
+    bit = 2
+    while bit < total:
+        part = part + swap(part, bit)
+        bit *= 2
+    other = swap(part, 1)
+    return jnp.where(
+        low == 0,
+        jnp.concatenate([part, other], 0),
+        jnp.concatenate([other, part], 0),
+    )
+
+
 def on_device(precip, thresholds, bin_index, test_matrix):
     highest = lax.Precision.HIGHEST
     tm_count = lax.axis_size("tm")
@@ -53,12 +87,12 @@
     excess = jnp.maximum(anomaly - level_own[None, :], 0.0)
     sketch = lax.dot_general(
         excess,
-        lax.all_gather(test_matrix, "tm", axis=0, tiled=True),
+        all_days(test_matrix, tm_count, tm_place, lax.axis_size("pts")),
         (((0,), (0,)), ((), ())),
         precision=highest,
     )
     local_cross = jnp.dot(sketch.T, sketch, precision=highest)
-    cross = lax.psum(local_cross, ("tm", "pts")) / points_total
+    cross = sum_all(local_cross) / points_total
     lower = jnp.linalg.cholesky(cross)
     basis = lax.linalg.triangular_solve(
         lower, sketch, left_side=False, lower=True, transpose_a=True

time: 240 us -> 124 us (0.52)
  waiting for transfers between devices: 127 us -> 30.4 us
  blocking collectives: 13.6 us -> 0 us
  between operations: 15.6 us -> 2.3 us
  starting transfers between devices: 4.26 us -> 14.2 us
    psum x1 -> x0, waiting for transfers between devices: 127 us -> none  [on_device(): cross = lax.psum(local_cross, ('tm', 'pts')) / points_total]
    ppermute x0 -> x7, waiting for transfers between devices: none -> 30.4 us  [swap(): return lax.ppermute(value, AXES, [(i, i ^ bit) for i in range(total)])]
    all_gather x1 -> x0, blocking collectives: 13.6 us -> none  [on_device(): lax.all_gather(test_matrix, 'tm', axis=0, tiled=True)]
    ppermute x0 -> x7, starting transfers between devices: none -> 9.77 us  [swap(): return lax.ppermute(value, AXES, [(i, i ^ bit) for i in range(total)])]
    unnamed x11 -> x9, local copies, waits for them, and re-layouts: 5.9 us -> 4.38 us
  transfers between devices with their start and end apart: 2 -> 8, of which waited for: 1 -> 7; matrix products, arithmetic and copies ran while one was open for 2% -> 5% of each run, Pallas kernels for 0% -> 0%
where the time goes in v1:
time: 124 us
  other arithmetic  59.6 us (48%)
  waiting for transfers between devices  30.4 us (25%)
  starting transfers between devices  14.2 us (11%)
  local copies, waits for them, and re-layouts  9.85 us (8%)
  matrix products  7.48 us (6%)
  between operations  2.3 us (2%)
    another operation x7, other arithmetic, on_device(): lower = jnp.linalg.cholesky(cross)  34.8 us
    ppermute x7, waiting for transfers between devices, swap(): return lax.ppermute(value, AXES, [(i, i ^ bit) for i in range(total)])  30.4 us
    another operation x3, other arithmetic, on_device(): lax.linalg.triangular_solve(lower, sketch, left_side=False, lower=True, t...  19.7 us
    ppermute x7, starting transfers between devices, swap(): return lax.ppermute(value, AXES, [(i, i ^ bit) for i in range(total)])  9.77 us
    all_to_all x1, starting transfers between devices, on_device(): lax.all_to_all(precip, 'tm', split_axis=1, concat_axis=0, tiled=True)  4.39 us
    unnamed x9, local copies, waits for them, and re-layouts  4.38 us
    another operation x6, local copies, waits for them, and re-layouts  4.02 us
  transfers between devices with their start and end apart: 8, of which 7 were waited for; matrix products, arithmetic and copies ran while one was open for 5% of the time, Pallas kernels for 0%

profile of v1, /device:TPU:0, one launch (start us, length us, event | category | flops | bytes accessed | tf_op | source)
XLA Modules:
  0.0 123.8 jit_solution(3260924505696430201)
XLA Ops:
  0.6 2.5 %copy.18 = f32[256,1024]{0,1:T(8,128)} copy(f32[256,1024]{1,0:T(8,128)} %param.4) | data formatting | bytes 2097152 | tf_op args[0]
  3.2 4.4 %all-to-all-start = ((f32[256,2,512]{0,2,1:T(8,128)}), f32[256,2,512]{0,2,1:T(8,128)S(1)}, u32[]{:S(2)}, u32[]{:S(2)}) async-start(f32[256,2,512]{0,2,1:T(8,128)} %bitcast), calls=%async_computation | async-start | bytes 2097152 | tf_op jit(solution)/shard_map/all_to_all | solution.py:80
  7.6 2.4 %collective-permute-start = (f32[256,256]{1,0:T(8,128)S(1)}, f32[256,256]{1,0:T(8,128)S(1)}, u32[]{:S(2)}, u32[]{:S(2)}) collective-permute-start(f32[256,256]{1,0:T(8,128)S(1)} %copy-done.1), channel_id=1, source_target_pairs={{0,16},{1,17},{2,18},{3,19},{4,20},{5,21},{6,22},{7,23},{8,24},{9,... | collective-permute-start | bytes 786440 | tf_op jit(solution)/shard_map/ppermute | solution.py:36
  10.7 0.2 fusion.40
  10.9 0.1 copy.20
  11.0 1.5 %cholesky.60 = f32[17,17]{1,0:T(8,128)S(1)} custom-call(f32[17,17]{1,0:T(8,128)S(1)} %fusion.20), custom_call_target="Cholesky" | custom-call | tf_op jit(solution)/shard_map/jit(cholesky)/cholesky | solution.py:75
  12.6 0.6 compare_reduce_fusion.2
  13.2 0.7 fusion.15
  13.9 0.4 fusion.2
  14.4 1.3 %custom-call.22 = f32[1,17,17]{1,2,0:T(8,128)S(1)} custom-call(f32[1,17,17]{2,1,0:T(8,128)S(1)} %fusion.15), custom_call_target="InvertDiagBlocksLowerTriangular" | custom-call | tf_op jit(solution)/shard_map/triangular_solve | solution.py:26
  15.8 11.8 %collective-permute-done = f32[256,256]{1,0:T(8,128)S(1)} collective-permute-done((f32[256,256]{1,0:T(8,128)S(1)}, f32[256,256]{1,0:T(8,128)S(1)}, u32[]{:S(2)}, u32[]{:S(2)}) %collective-permute-start) | collective-permute-done | bytes 262176 | tf_op jit(solution)/shard_map/ppermute | solution.py:36
  27.7 0.6 gather_fusion
  28.3 0.3 copy.19
  28.6 0.6 fusion.41
  29.2 0.2 fusion.18
  29.5 0.2 fusion.16
  29.7 1.1 fusion.1
  30.8 1.8 %fusion.42 = f32[512,256]{1,0:T(8,128)S(1)} fusion(f32[512,512]{1,0:T(8,128)S(1)} %fusion.1, f32[512,256]{1,0:T(8,128)S(1)} %bitcast.71), kind=kOutput, calls=%fused_computation.85 | convolution fusion | flops 805306368 | bytes 2097152 | tf_op jit(solution)/shard_map/dot_general | solution.py:88
  32.6 1.0 fusion.43
  33.8 1.3 %collective-permute-done.1 = f32[128,256]{0,1:T(8,128)S(1)} collective-permute-done((f32[128,256]{0,1:T(8,128)S(1)}, f32[128,256]{0,1:T(8,128)S(1)}, u32[]{:S(2)}, u32[]{:S(2)}) %collective-permute-start.1) | collective-permute-done | bytes 131104 | tf_op jit(solution)/shard_map/ppermute | solution.py:36
  35.1 1.8 %collective-permute-start.2 = (f32[128,256]{0,1:T(8,128)S(1)}, f32[128,256]{0,1:T(8,128)S(1)}, u32[]{:S(2)}, u32[]{:S(2)}) collective-permute-start(f32[128,256]{0,1:T(8,128)S(1)} %dynamic-slice_add_fusion), channel_id=1, source_target_pairs={{0,2},{1,3},{2,0},{3,1},{4,6},{5,7},{6,4},{7,5},{8,10},{9,11},{10,... | collective-permute-start | bytes 393224 | tf_op jit(solution)/shard_map/ppermute | solution.py:36
  36.9 3.8 %collective-permute-done.2 = f32[128,256]{0,1:T(8,128)S(1)} collective-permute-done((f32[128,256]{0,1:T(8,128)S(1)}, f32[128,256]{0,1:T(8,128)S(1)}, u32[]{:S(2)}, u32[]{:S(2)}) %collective-permute-start.2) | collective-permute-done | bytes 131104 | tf_op jit(solution)/shard_map/ppermute | solution.py:36
  40.7 1.9 %collective-permute-start.3 = (f32[128,256]{0,1:T(8,128)S(1)}, f32[128,256]{0,1:T(8,128)S(1)}, u32[]{:S(2)}, u32[]{:S(2)}) collective-permute-start(f32[128,256]{0,1:T(8,128)S(1)} %add.80), channel_id=1, source_target_pairs={{0,4},{1,5},{2,6},{3,7},{4,0},{5,1},{6,2},{7,3},{8,12},{9,13},{10,... | collective-permute-start | bytes 393224 | tf_op jit(solution)/shard_map/ppermute | solution.py:36
  42.6 3.2 %collective-permute-done.3 = f32[128,256]{0,1:T(8,128)S(1)} collective-permute-done((f32[128,256]{0,1:T(8,128)S(1)}, f32[128,256]{0,1:T(8,128)S(1)}, u32[]{:S(2)}, u32[]{:S(2)}) %collective-permute-start.3) | collective-permute-done | bytes 131104 | tf_op jit(solution)/shard_map/ppermute | solution.py:36
  45.8 2.9 %collective-permute-start.4 = (f32[128,256]{0,1:T(8,128)S(1)}, f32[128,256]{0,1:T(8,128)S(1)}, u32[]{:S(2)}, u32[]{:S(2)}) collective-permute-start(f32[128,256]{0,1:T(8,128)S(1)} %add.81), channel_id=1, source_target_pairs={{0,8},{1,9},{2,10},{3,11},{4,12},{5,13},{6,14},{7,15},{8,0},{9,1},... | collective-permute-start | bytes 393224 | tf_op jit(solution)/shard_map/ppermute | solution.py:36
  48.7 4.6 %collective-permute-done.4 = f32[128,256]{0,1:T(8,128)S(1)} collective-permute-done((f32[128,256]{0,1:T(8,128)S(1)}, f32[128,256]{0,1:T(8,128)S(1)}, u32[]{:S(2)}, u32[]{:S(2)}) %collective-permute-start.4) | collective-permute-done | bytes 131104 | tf_op jit(solution)/shard_map/ppermute | solution.py:36
  53.3 0.7 collective-permute-start.5
  54.0 4.3 %collective-permute-done.5 = f32[128,256]{0,1:T(8,128)S(1)} collective-permute-done((f32[128,256]{0,1:T(8,128)S(1)}, f32[128,256]{0,1:T(8,128)S(1)}, u32[]{:S(2)}, u32[]{:S(2)}) %collective-permute-start.5) | collective-permute-done | bytes 131104 | tf_op jit(solution)/shard_map/ppermute | solution.py:36
  58.4 1.3 %collective-permute-done.6 = f32[128,256]{0,1:T(8,128)S(1)} collective-permute-done((f32[128,256]{0,1:T(8,128)S(1)}, f32[128,256]{0,1:T(8,128)S(1)}, u32[]{:S(2)}, u32[]{:S(2)}) %collective-permute-start.6) | collective-permute-done | bytes 131104 | tf_op jit(solution)/shard_map/ppermute | solution.py:36
  59.8 0.1 copy.23
  60.0 11.7 %cholesky.123 = f32[128,128]{1,0:T(8,128)S(1)} custom-call(f32[128,128]{1,0:T(8,128)S(1)} %cholesky.153), custom_call_target="Cholesky" | custom-call | tf_op jit(solution)/shard_map/jit(cholesky)/cholesky | solution.py:96
  71.8 10.0 %custom-call.23 = f32[1,128,128]{1,2,0:T(8,128)S(1)} custom-call(f32[1,128,128]{2,1,0:T(8,128)S(1)} %get-tuple-element.31), custom_call_target="InvertDiagBlocksLowerTriangular" | custom-call | tf_op jit(solution)/shard_map/jit(cholesky)/cholesky | solution.py:96
  81.7 0.2 constant_dynamic-update-slice_fusion
  81.9 0.3 convolution_subtract_fusion.2
  82.2 11.7 %cholesky.140 = f32[128,128]{1,0:T(8,128)S(1)} custom-call(f32[128,128]{1,0:T(8,128)S(1)} %convolution_subtract_fusion.2), custom_call_target="Cholesky" | custom-call | tf_op jit(solution)/shard_map/jit(cholesky)/cholesky | solution.py:96
  93.9 0.7 compare_reduce_fusion
  94.7 0.6 compare_reduce_fusion.1
  96.7 4.1 %while.1 = (s32[]{:T(128)}, f32[256,256]{1,0:T(8,128)S(1)}, s32[2,2]{1,0:T(2,128)S(1)}, f32[2,128,128]{2,1,0:T(8,128)S(1)}, s32[]{:T(128)}) while((s32[]{:T(128)}, f32[256,256]{1,0:T(8,128)S(1)}, s32[2,2]{1,0:T(2,128)S(1)}, f32[2,128,128]{2,1,0:T(8,128)S(1)}, s32[]{:T(128)}) %tuple.38), condition=%wide.while_cond, body=%wide.while_body.sunk | while | flops 2 | bytes 131181 | solution.py:97
  96.7 0.6 fusion.61
  97.3 1.4 %bitcast_dynamic-update-slice_fusion.2 = f32[2,128,128]{2,1,0:T(8,128)S(1)} fusion(f32[2,128,128]{2,1,0:T(8,128)S(1)} %get-tuple-element.87, s32[]{:T(128)} %get-tuple-element.84, f32[256,256]{1,0:T(8,128)S(1)} %get-tuple-element.90, s32[]{:T(128)} %bitcast.66, s32[]{:T(128)} %bitcast.67), kind=kLoop, calls=%fused_computation.1.clone.1 | loop fusion | bytes 131084 | tf_op jit(solution)/shard_map/triangular_solve
  98.8 0.6 fusion.61
  99.4 1.4 %bitcast_dynamic-update-slice_fusion.2 = f32[2,128,128]{2,1,0:T(8,128)S(1)} fusion(f32[2,128,128]{2,1,0:T(8,128)S(1)} %get-tuple-element.87, s32[]{:T(128)} %get-tuple-element.84, f32[256,256]{1,0:T(8,128)S(1)} %get-tuple-element.90, s32[]{:T(128)} %bitcast.66, s32[]{:T(128)} %bitcast.67), kind=kLoop, calls=%fused_computation.1.clone.1 | loop fusion | bytes 131084 | tf_op jit(solution)/shard_map/triangular_solve
  100.8 19.7 %custom-call.24 = f32[2,128,128]{1,2,0:T(8,128)S(1)} custom-call(f32[2,128,128]{2,1,0:T(8,128)S(1)} %get-tuple-element.9), custom_call_target="InvertDiagBlocksLowerTriangular" | custom-call | tf_op jit(solution)/shard_map/triangular_solve | solution.py:97
  120.5 0.4 fusion.3
  120.9 0.6 convolution_subtract_fusion.1
  121.5 0.4 fusion.10
  122.0 1.0 copy.24
  123.0 0.8 copy.25
  (44 shorter events, 1.5 us)
Async XLA Ops:
  0.6 13.3 %copy-start = (f32[64]{0:T(128)S(1)}, f32[64]{0:T(128)}, u32[]{:S(2)}) copy-start(f32[64]{0:T(128)} %param.5) | copy-start | bytes 772
  3.2 4.4 %copy-start.1 = (f32[256,256]{1,0:T(8,128)S(1)}, f32[256,256]{1,0:T(8,128)}, u32[]{:S(2)}) copy-start(f32[256,256]{1,0:T(8,128)} %param.7) | copy-start | bytes 786436
  3.2 25.1 %all-to-all-start = ((f32[256,2,512]{0,2,1:T(8,128)}), f32[256,2,512]{0,2,1:T(8,128)S(1)}, u32[]{:S(2)}, u32[]{:S(2)}) async-start(f32[256,2,512]{0,2,1:T(8,128)} %bitcast), calls=%async_computation | async-start | bytes 2097152 | tf_op jit(solution)/shard_map/all_to_all | solution.py:80
  7.6 20.0 %collective-permute-start = (f32[256,256]{1,0:T(8,128)S(1)}, f32[256,256]{1,0:T(8,128)S(1)}, u32[]{:S(2)}, u32[]{:S(2)}) collective-permute-start(f32[256,256]{1,0:T(8,128)S(1)} %copy-done.1), channel_id=1, source_target_pairs={{0,16},{1,17},{2,18},{3,19},{4,20},{5,21},{6,22},{7,23},{8,24},{9,... | collective-permute-start | bytes 786440 | tf_op jit(solution)/shard_map/ppermute | solution.py:36
  13.2 0.7 copy-start.2
  33.7 1.4 %collective-permute-start.1 = (f32[128,256]{0,1:T(8,128)S(1)}, f32[128,256]{0,1:T(8,128)S(1)}, u32[]{:S(2)}, u32[]{:S(2)}) collective-permute-start(f32[128,256]{0,1:T(8,128)S(1)} %constant_dynamic-slice_fusion.1), channel_id=1, source_target_pairs={{0,1},{1,0},{2,3},{3,2},{4,5},{5,4},{6,7},{7,6},{8,9},{9,8},{10,11... | collective-permute-start | bytes 393224 | tf_op jit(solution)/shard_map/ppermute | solution.py:36
  35.1 5.6 %collective-permute-start.2 = (f32[128,256]{0,1:T(8,128)S(1)}, f32[128,256]{0,1:T(8,128)S(1)}, u32[]{:S(2)}, u32[]{:S(2)}) collective-permute-start(f32[128,256]{0,1:T(8,128)S(1)} %dynamic-slice_add_fusion), channel_id=1, source_target_pairs={{0,2},{1,3},{2,0},{3,1},{4,6},{5,7},{6,4},{7,5},{8,10},{9,11},{10,... | collective-permute-start | bytes 393224 | tf_op jit(solution)/shard_map/ppermute | solution.py:36
  40.7 5.0 %collective-permute-start.3 = (f32[128,256]{0,1:T(8,128)S(1)}, f32[128,256]{0,1:T(8,128)S(1)}, u32[]{:S(2)}, u32[]{:S(2)}) collective-permute-start(f32[128,256]{0,1:T(8,128)S(1)} %add.80), channel_id=1, source_target_pairs={{0,4},{1,5},{2,6},{3,7},{4,0},{5,1},{6,2},{7,3},{8,12},{9,13},{10,... | collective-permute-start | bytes 393224 | tf_op jit(solution)/shard_map/ppermute | solution.py:36
  45.8 7.5 %collective-permute-start.4 = (f32[128,256]{0,1:T(8,128)S(1)}, f32[128,256]{0,1:T(8,128)S(1)}, u32[]{:S(2)}, u32[]{:S(2)}) collective-permute-start(f32[128,256]{0,1:T(8,128)S(1)} %add.81), channel_id=1, source_target_pairs={{0,8},{1,9},{2,10},{3,11},{4,12},{5,13},{6,14},{7,15},{8,0},{9,1},... | collective-permute-start | bytes 393224 | tf_op jit(solution)/shard_map/ppermute | solution.py:36
  53.3 5.0 %collective-permute-start.5 = (f32[128,256]{0,1:T(8,128)S(1)}, f32[128,256]{0,1:T(8,128)S(1)}, u32[]{:S(2)}, u32[]{:S(2)}) collective-permute-start(f32[128,256]{0,1:T(8,128)S(1)} %add.82), channel_id=1, source_target_pairs={{0,16},{1,17},{2,18},{3,19},{4,20},{5,21},{6,22},{7,23},{8,24},{9,... | collective-permute-start | bytes 393224 | tf_op jit(solution)/shard_map/ppermute | solution.py:36
  58.3 1.4 %collective-permute-start.6 = (f32[128,256]{0,1:T(8,128)S(1)}, f32[128,256]{0,1:T(8,128)S(1)}, u32[]{:S(2)}, u32[]{:S(2)}) collective-permute-start(f32[128,256]{0,1:T(8,128)S(1)} %add.83), channel_id=1, source_target_pairs={{0,1},{1,0},{2,3},{3,2},{4,5},{5,4},{6,7},{7,6},{8,9},{9,8},{10,11... | collective-permute-start | bytes 393224 | tf_op jit(solution)/shard_map/ppermute | solution.py:36

commit v2 on v0

v2 whole, which is shorter than its diff:
```python
import functools
import math

import jax
import jax.numpy as jnp
import numpy as np
from jax import lax
from jax.experimental import pallas as pl
from jax.experimental.pallas import tpu as pltpu
from jax.sharding import PartitionSpec as P

HARM = 8
SUB = 8
AXES = ("tm", "pts")
HI = lax.Precision.HIGHEST

year_days = 365.25


def harmonic_filter(days_total):
    phase_base = np.arange(days_total).astype(np.float32)
    columns = [np.ones_like(phase_base)]
    for order in range(1, HARM + 1):
        phase = np.float32(2.0 * math.pi * order / year_days) * phase_base
        columns.append(np.cos(phase.astype(np.float64)))
        columns.append(np.sin(phase.astype(np.float64)))
    table = np.stack(columns, 0).astype(np.float32).astype(np.float64)
    low = np.linalg.cholesky(table @ table.T)
    rows = np.linalg.solve(low, table)
    padded = -(-rows.shape[0] // SUB) * SUB
    rows = np.concatenate([rows, np.zeros((padded - rows.shape[0], days_total))], 0)
    return rows.astype(np.float32)


def nn(a, b):
    return jnp.dot(a, b, precision=HI, preferred_element_type=jnp.float32)


def nt(a, b):
    return lax.dot_general(
        a, b, (((1,), (1,)), ((), ())), precision=HI, preferred_element_type=jnp.float32
    )


def tn(a, b):
    return lax.dot_general(
        a, b, (((0,), (0,)), ((), ())), precision=HI, preferred_element_type=jnp.float32
    )


def swap(value, bit):
    total = lax.axis_size("tm") * lax.axis_size("pts")
    return lax.ppermute(value, AXES, [(i, i ^ bit) for i in range(total)])


def front_kernel(start, own_rows, tm_count, first, last, *refs):
    refs = list(refs)
    take = lambda n: [refs.pop(0) for _ in range(n)]
    (days_ref, thr_ref, bin_ref, filt_ref, filt_t_ref, test_ref) = take(6)
    recv_refs = take(tm_count - 1)
    half_refs = take(2 * (tm_count - 1))
    acc_ref = None if first else take(1)[0]
    sketch_ref = take(1)[0]
    outs = take(2) if last else take(1)
    own_ref, table_ref, sem = take(3)
    width = own_ref.shape[1]
    days_local = own_ref.shape[0]
    place = lax.axis_index("tm")
    low = lax.axis_index("pts") % 2
    at = pl.multiple_of(place * own_rows + start, math.gcd(own_rows, start) if start else own_rows)
    copy = pltpu.make_async_copy(days_ref.at[:, pl.ds(at, width)], own_ref, sem)
    copy.start()
    table_ref[:days_local, :] = test_ref[...]
    half = days_local // 2
    for k in range(tm_count - 1):
        base = days_local * (k + 1)
        table_ref[pl.ds(pl.multiple_of(base + low * half, half), half), :] = half_refs[2 * k][...]
        table_ref[pl.ds(pl.multiple_of(base + (1 - low) * half, half), half), :] = half_refs[2 * k + 1][...]
    bins = bin_ref[:, pl.ds(at, width)]
    count = thr_ref.shape[0]
    entry = lax.broadcasted_iota(jnp.int32, (count, width), 0)
    level = jnp.sum(jnp.where(entry == bins, thr_ref[...], 0.0), axis=0, keepdims=True)
    copy.wait()
    series = [own_ref[...]] + [r[...] for r in recv_refs]
    proj = nn(filt_ref[place], series[0])
    for k in range(1, tm_count):
        proj = proj + nn(filt_ref[place ^ k], series[k])
    excess = [
        jnp.maximum(series[k] - nn(filt_t_ref[place ^ k], proj) - level, 0.0)
        for k in range(tm_count)
    ]
    sketch = tn(jnp.concatenate(excess, 0), table_ref[...])
    sketch_ref[...] = sketch
    cross = tn(sketch, sketch)
    if not first:
        cross = cross + acc_ref[...]
    if not last:
        outs[0][...] = cross
        return
    kept_ref, sent_ref = outs
    tile = cross.shape[0] // 2
    row = lax.broadcasted_iota(jnp.int32, (tile, tile), 0)
    col = lax.broadcasted_iota(jnp.int32, (tile, tile), 1)
    second = cross[tile:, tile:]
    ends = jnp.where(row >= col, cross[:tile, :tile], second)
    side = cross[tile:, :tile]
    diag = jnp.broadcast_to(
        jnp.sum(jnp.where(row == col, second, 0.0), axis=0, keepdims=True), (SUB, tile)
    )
    kept_ref[:tile, :] = jnp.where(low == 0, ends, side)
    sent_ref[:tile, :] = jnp.where(low == 0, side, ends)
    kept_ref[tile:, :] = diag
    sent_ref[tile:, :] = diag


def over_lanes(value, col, tile):
    return jnp.broadcast_to(value[:, col:col + 1], (SUB, tile))


def over_rows(value, row, tile):
    return jnp.broadcast_to(value[row:row + 1, :], (SUB, tile))


def panel(blocks):
    count = len(blocks)
    blocks = list(blocks)
    tile = count * SUB
    lane = lax.broadcasted_iota(jnp.int32, (SUB, tile), 1)
    row = lax.broadcasted_iota(jnp.int32, (SUB, tile), 0)
    upper, inverse = [], []
    for i in range(count):
        first = SUB * i
        own = blocks[i]
        cols = [over_lanes(own, first + k, tile) for k in range(SUB)]
        e = {(j, k): over_rows(cols[k], j, tile) for k in range(SUB) for j in range(k + 1)}
        inside = (lane >= first) & (lane < first + SUB)
        later = {
            t: [over_lanes(blocks[t], first + k, tile) for k in range(SUB)]
            for t in range(i + 1, count)
        }
        rows = [
            jnp.where(inside, jnp.where(lane == first + j, 1.0, 0.0), over_rows(own, j, tile))
            for j in range(SUB)
        ]
        for j in range(SUB):
            s = lax.rsqrt(e[j, j])
            fac = {k: e[j, k] * s for k in range(j + 1, SUB)}
            e[j, j] = e[j, j] * s
            rows[j] = rows[j] * s
            for t in later:
                later[t][j] = later[t][j] * s
            for k in range(j + 1, SUB):
                e[j, k] = fac[k]
                for m in range(k, SUB):
                    e[k, m] = e[k, m] - fac[k] * fac[m]
                rows[k] = rows[k] - fac[k] * rows[j]
                for t in later:
                    later[t][k] = later[t][k] - fac[k] * later[t][j]
        for t in later:
            terms = [later[t][j] * rows[j] for j in range(SUB)]
            while len(terms) > 1:
                terms = [terms[q] + terms[q + 1] for q in range(0, len(terms), 2)]
            blocks[t] = jnp.where(inside, 0.0, blocks[t]) - terms[0]
        up = jnp.zeros((SUB, tile), jnp.float32)
        inv = up
        for j in range(SUB):
            line = jnp.where(lane >= first + SUB, rows[j], 0.0)
            for k in range(j, SUB):
                line = jnp.where(lane == first + k, e[j, k], line)
            up = jnp.where(row == j, line, up)
            inv = jnp.where(row == j, rows[j], inv)
        upper.append(up)
        inverse.append(jnp.where(lane < first + SUB, inv, 0.0))
    return jnp.concatenate(upper, 0), jnp.concatenate(inverse, 0)


def back_kernel(points_total, chunks, part_ref, other_ref, *refs):
    sketch_refs = refs[:chunks]
    basis_ref, factor_ref = refs[chunks:]
    tile = part_ref.shape[1]
    low = lax.axis_index("pts") % 2
    part = part_ref[...] / points_total
    other = other_ref[...] / points_total
    ends = jnp.where(low == 0, part[:tile], other[:tile])
    side = jnp.where(low == 0, other[:tile], part[:tile])
    diag = jnp.where(low == 0, other[tile:tile + 1], part[tile:tile + 1])
    row = lax.broadcasted_iota(jnp.int32, (tile, tile), 0)
    col = lax.broadcasted_iota(jnp.int32, (tile, tile), 1)
    ends_t = ends.T
    side_t = side.T
    split = lambda a: [a[SUB * t:SUB * (t + 1), :] for t in range(tile // SUB)]
    up, inv1 = panel(split(jnp.where(row >= col, ends, ends_t)))
    factor_ref[:tile, :tile] = up
    factor_ref[tile:, :tile] = jnp.zeros((tile, tile), jnp.float32)
    right = nn(inv1, side_t)
    right_t = nt(side, inv1)
    factor_ref[:tile, tile:] = right
    rest = jnp.where(row < col, ends, jnp.where(row == col, diag, ends_t)) - nn(right_t, right)
    up, inv2 = panel(split(rest))
    factor_ref[tile:, tile:] = up
    at = 0
    for ref in sketch_refs:
        size = ref.shape[0]
        left = nt(ref[:, :tile], inv1)
        basis_ref[at:at + size, :tile] = left
        basis_ref[at:at + size, tile:] = nt(ref[:, tile:] - nn(left, right), inv2)
        at += size


def chunk_widths(own_rows):
    last = own_rows // 4
    if last % 128:
        return [own_rows]
    return [own_rows - last, last]


def on_device(precip, thresholds, bin_index, test_matrix):
    tm_count = lax.axis_size("tm")
    pts_count = lax.axis_size("pts")
    place = lax.axis_index("tm")
    low = lax.axis_index("pts") % 2
    days_local, points_local = precip.shape
    columns = test_matrix.shape[1]
    tile = columns // 2
    own_rows = points_local // tm_count
    days_total = days_local * tm_count
    points_total = points_local * pts_count
    f32 = jnp.float32

    rows = harmonic_filter(days_total)
    filt = rows.reshape(rows.shape[0], tm_count, days_local).transpose(1, 0, 2)
    filt_t = jnp.asarray(filt.transpose(0, 2, 1))
    filt = jnp.asarray(filt)
    thr = thresholds[:, None]
    bins = bin_index[None, :]

    half = days_local // 2
    mine = lax.dynamic_slice_in_dim(test_matrix, low * half, half, 0)
    halves = []
    for k in range(1, tm_count):
        halves.append(swap(mine, k * pts_count))
    halves = [h for got in halves for h in (got, swap(got, 1))]

    vmem = pl.BlockSpec(memory_space=pltpu.VMEM)
    start = 0
    widths = chunk_widths(own_rows)
    received = []
    for width in widths:
        received.append(
            [
                swap(
                    lax.dynamic_slice_in_dim(precip, (place ^ k) * own_rows + start, width, 1),
                    k * pts_count,
                )
                for k in range(1, tm_count)
            ]
        )
        start += width

    sketches = []
    cross = None
    start = 0
    for index, width in enumerate(widths):
        first, last = index == 0, index == len(widths) - 1
        operands = [precip, thr, bins, filt, filt_t, test_matrix] + received[index] + halves
        specs = [pl.BlockSpec(memory_space=pl.ANY)] + [vmem] * (len(operands) - 1)
        if not first:
            operands.append(cross)
            specs.append(vmem)
        shapes = [jax.ShapeDtypeStruct((width, columns), f32)]
        if last:
            shapes += [jax.ShapeDtypeStruct((tile + SUB, tile), f32)] * 2
        else:
            shapes += [jax.ShapeDtypeStruct((columns, columns), f32)]
        out = pl.pallas_call(
            functools.partial(front_kernel, start, own_rows, tm_count, first, last),
            out_shape=shapes,
            in_specs=specs,
            out_specs=[vmem] * len(shapes),
            scratch_shapes=[
                pltpu.VMEM((days_local, width), f32),
                pltpu.VMEM((days_total, columns), f32),
                pltpu.SemaphoreType.DMA,
            ],
            cost_estimate=pl.CostEstimate(
                flops=12 * width * columns * (days_total + columns),
                bytes_accessed=4 * days_total * (width + columns),
                transcendentals=0,
            ),
            name=f"front{index}",
        )(*operands)
        sketches.append(out[0])
        cross = out[1]
        start += width
    kept, sent = out[1], out[2]

    part = kept + swap(sent, 1)
    bit = 2
    while bit < tm_count * pts_count:
        part = part + swap(part, bit)
        bit *= 2
    other = swap(part, 1)

    basis, factor = pl.pallas_call(
        functools.partial(back_kernel, points_total, len(sketches)),
        out_shape=(
            jax.ShapeDtypeStruct((own_rows, columns), f32),
            jax.ShapeDtypeStruct((columns, columns), f32),
        ),
        in_specs=[vmem] * (2 + len(sketches)),
        out_specs=(vmem, vmem),
        name="back",
    )(part, other, *sketches)
    return basis, factor


def solution(mesh):
    in_specs = (P("tm", "pts"), P(), P("pts"), P("tm", None))
    out_specs = (P(("pts", "tm"), None), P())
    return jax.shard_map(
        on_device, mesh=mesh, in_specs=in_specs, out_specs=out_specs, check_vma=False
    )
```

time: 240 us -> 68.1 us (0.28)
  waiting for transfers between devices: 127 us -> 26 us
  other arithmetic: 60.4 us -> 0.93 us
  Pallas kernels: 0 us -> 23.2 us
  between operations: 15.6 us -> 0.76 us
  blocking collectives: 13.6 us -> 0 us
  matrix products: 8.22 us -> 0 us
  starting transfers between devices: 4.26 us -> 12 us
  local copies, waits for them, and re-layouts: 10.7 us -> 4.81 us
    psum x1 -> x0, waiting for transfers between devices: 127 us -> none  [on_device(): cross = lax.psum(local_cross, ('tm', 'pts')) / points_total]
    another operation x15 -> x0, other arithmetic: 58.7 us -> none  [the longest x7 34.8 us: on_device(): lower = jnp.linalg.cholesky(cross)]
    ppermute x0 -> x10, waiting for transfers between devices: none -> 26 us  [swap(): return lax.ppermute(value, AXES, [(i, i ^ bit) for i in range(total)])]
    pallas_call x0 -> x3, Pallas kernels: none -> 23.2 us  [the longest x1 12.3 us: on_device(): pl.pallas_call(functools.partial(back_kernel, points_total, len(sketches)...]
    all_gather x1 -> x0, blocking collectives: 13.6 us -> none  [on_device(): lax.all_gather(test_matrix, 'tm', axis=0, tiled=True)]
    ppermute x0 -> x10, starting transfers between devices: none -> 12 us  [swap(): return lax.ppermute(value, AXES, [(i, i ^ bit) for i in range(total)])]
    dot_general x6 -> x0, matrix products: 5.91 us -> none  [the longest x1 1.85 us: on_device(): lax.dot_general(excess, lax.all_gather(test_matrix, 'tm', axis=0, tiled=T...]
    all_to_all x1 -> x0, starting transfers between devices: 4.26 us -> none  [on_device(): lax.all_to_all(precip, 'tm', split_axis=1, concat_axis=0, tiled=True)]
  transfers between devices with their start and end apart: 2 -> 10, of which waited for: 1 -> 7; matrix products, arithmetic and copies ran while one was open for 2% -> 2% of each run, Pallas kernels for 0% -> 9%
where the time goes in v2:
time: 68.1 us; the launch traced here: 67.8 us
  waiting for transfers between devices  26 us (38%)
  Pallas kernels  23.2 us (34%)
  starting transfers between devices  12 us (18%)
  local copies, waits for them, and re-layouts  4.81 us (7%)
  other arithmetic  0.93 us (1%)
  between operations  0.76 us (1%)
    ppermute x10, waiting for transfers between devices, swap(): return lax.ppermute(value, AXES, [(i, i ^ bit) for i in range(total)])  26 us
    pallas_call x1, Pallas kernels, on_device(): pl.pallas_call(functools.partial(back_kernel, points_total, len(sketches)...  12.3 us
    ppermute x10, starting transfers between devices, swap(): return lax.ppermute(value, AXES, [(i, i ^ bit) for i in range(total)])  12 us
    pallas_call x2, Pallas kernels, on_device(): pl.pallas_call(functools.partial(front_kernel, start, own_rows, tm_count,...  10.9 us
    unnamed x16, local copies, waits for them, and re-layouts  2.07 us
    dynamic_slice x2, local copies, waits for them, and re-layouts, on_device(): lax.dynamic_slice_in_dim(precip, (place ^ k) * own_rows + start, width, 1)  2.03 us
  transfers between devices with their start and end apart: 10, of which 7 were waited for; matrix products, arithmetic and copies ran while one was open for 2% of the time, Pallas kernels for 9%

profile of v2, /device:TPU:0, one launch (start us, length us, event | category | flops | bytes accessed | tf_op | source)
XLA Modules:
  0.0 67.8 jit_solution(8197309899772699205)
XLA Ops:
  0.6 0.0 copy-start
  0.7 1.1 %constant_dynamic-slice_fusion = f32[256,384]{1,0:T(8,128)S(1)} fusion(f32[256,1024]{1,0:T(8,128)} %refs_0_.3, s32[]{:T(128)S(6)} %select_n.19), kind=kLoop, calls=%fused_computation | loop fusion | bytes 786436 | tf_op jit(solution)/shard_map/dynamic_slice | solution.py:252
  1.7 3.1 %collective-permute-start.3 = (f32[256,384]{1,0:T(8,128)S(1)}, f32[256,384]{1,0:T(8,128)S(1)}, u32[]{:S(2)}, u32[]{:S(2)}) collective-permute-start(f32[256,384]{1,0:T(8,128)S(1)} %constant_dynamic-slice_fusion), channel_id=1, source_target_pairs={{0,16},{1,17},{2,18},{3,19},{4,20},{5,21},{6,22},{7,23},{8,24},{9,... | collective-permute-start | bytes 1179656 | tf_op jit(solution)/shard_map/ppermute | solution.py:53
  4.8 0.0 copy-done
  4.8 0.1 collective-permute-start.1
  4.9 11.8 %collective-permute-done.1.refs_7_ = f32[128,256]{1,0:T(8,128)S(1)} collective-permute-done((f32[128,256]{1,0:T(8,128)S(1)}, f32[128,256]{1,0:T(8,128)S(1)}, u32[]{:S(2)}, u32[]{:S(2)}) %collective-permute-start.1) | collective-permute-done | bytes 131104 | tf_op jit(solution)/shard_map/ppermute | solution.py:53
  16.7 0.0 copy-start.2
  16.7 0.0 collective-permute-start.2
  16.7 1.0 %constant_dynamic-slice_fusion.2 = f32[256,128]{1,0:T(8,128)S(1)} fusion(f32[256,1024]{1,0:T(8,128)} %refs_0_.3, s32[]{:T(128)S(6)} %select_n.16), kind=kLoop, calls=%fused_computation.2 | loop fusion | bytes 262148 | tf_op jit(solution)/shard_map/dynamic_slice | solution.py:252
  17.7 0.0 copy-done.2
  17.7 0.0 copy-start.6
  17.7 1.8 %collective-permute-start = (f32[256,128]{1,0:T(8,128)S(1)}, f32[256,128]{1,0:T(8,128)S(1)}, u32[]{:S(2)}, u32[]{:S(2)}) collective-permute-start(f32[256,128]{1,0:T(8,128)S(1)} %constant_dynamic-slice_fusion.2), channel_id=1, source_target_pairs={{0,16},{1,17},{2,18},{3,19},{4,20},{5,21},{6,22},{7,23},{8,24},{9,... | collective-permute-start | bytes 393224 | tf_op jit(solution)/shard_map/ppermute | solution.py:53
  19.5 0.0 copy-done.6
  19.5 0.7 %copy.9.refs_1_ = f32[64,1]{1,0:T(8,128)} copy(f32[64,1]{0,1:T(1,128)S(1)} %bitcast.4) | data formatting | bytes 512 | tf_op jit(solution)/shard_map/broadcast_in_dim | solution.py:234
  20.2 0.0 collective-permute-done.2.refs_8_
  20.2 0.0 copy-start.3
  20.2 0.0 collective-permute-done.3.refs_6_
  20.2 0.0 copy-start.7
  20.2 0.6 copy-done.3
  20.9 0.1 copy-done.7
  21.0 6.3 %front0.1 = (f32[384,256]{1,0:T(8,128)}, f32[256,256]{1,0:T(8,128)}) custom-call(f32[256,1024]{1,0:T(8,128)} %refs_0_.3, f32[64,1]{1,0:T(8,128)} %copy.9.refs_1_, s32[1,1024]{1,0:T(1,128)} %bitcast.2, f32[2,24,256]{2,1,0:T(8,128)} %constant.41.clone.refs_3_, f32[2,256,24]{2,1,0:T(8,128)} %constant.40.clone.refs_4_, f32[256,256]{1,0:T(8,128)} %refs_5_.3, ...), custom_call_target="tpu_custom_call" | custom-call | flops 905969664 | bytes 1310720 | tf_op jit(solution)/shard_map/front0/pallas_call | solution.py:275
  27.3 0.0 collective-permute-done.refs_6_
  27.3 0.0 copy-start.4
  27.3 0.6 copy-done.4
  28.0 4.6 %front1.1 = (f32[128,256]{1,0:T(8,128)}, f32[136,128]{1,0:T(8,128)}, f32[136,128]{1,0:T(8,128)}) custom-call(f32[256,1024]{1,0:T(8,128)} %refs_0_.3, f32[64,1]{1,0:T(8,128)} %copy.9.refs_1_, s32[1,1024]{1,0:T(1,128)} %bitcast.3, f32[2,24,256]{2,1,0:T(8,128)} %constant.41.clone.refs_3_, f32[2,256,24]{2,1,0:T(8,128)} %constant.40.clone.refs_4_, ...), custom_call_target="tpu_custom_call" | custom-call | flops 301989888 | bytes 786432 | tf_op jit(solution)/shard_map/front1/pallas_call | solution.py:275
  32.6 0.2 collective-permute-start.4
  32.9 1.3 %collective-permute-done.4 = f32[136,128]{1,0:T(8,128)S(1)} collective-permute-done((f32[136,128]{1,0:T(8,128)}, f32[136,128]{1,0:T(8,128)S(1)}, u32[]{:S(2)}, u32[]{:S(2)}) %collective-permute-start.4) | collective-permute-done | bytes 69664 | tf_op jit(solution)/shard_map/ppermute | solution.py:53
  34.2 0.9 %add.38 = f32[136,128]{1,0:T(8,128)S(1)} add(f32[136,128]{1,0:T(8,128)} %get-tuple-element.8, f32[136,128]{1,0:T(8,128)S(1)} %collective-permute-done.4) | non-fusion elementwise | flops 17408 | bytes 208896 | tf_op jit(solution)/shard_map/add | solution.py:297
  35.1 1.6 %collective-permute-start.5 = (f32[136,128]{1,0:T(8,128)S(1)}, f32[136,128]{1,0:T(8,128)S(1)}, u32[]{:S(2)}, u32[]{:S(2)}) collective-permute-start(f32[136,128]{1,0:T(8,128)S(1)} %add.38), channel_id=1, source_target_pairs={{0,2},{1,3},{2,0},{3,1},{4,6},{5,7},{6,4},{7,5},{8,10},{9,11},{10,... | collective-permute-start | bytes 208904 | tf_op jit(solution)/shard_map/ppermute | solution.py:53
  36.6 2.8 %collective-permute-done.5 = f32[136,128]{1,0:T(8,128)S(1)} collective-permute-done((f32[136,128]{1,0:T(8,128)S(1)}, f32[136,128]{1,0:T(8,128)S(1)}, u32[]{:S(2)}, u32[]{:S(2)}) %collective-permute-start.5) | collective-permute-done | bytes 69664 | tf_op jit(solution)/shard_map/ppermute | solution.py:53
  39.4 1.6 %collective-permute-start.6 = (f32[136,128]{1,0:T(8,128)S(1)}, f32[136,128]{1,0:T(8,128)S(1)}, u32[]{:S(2)}, u32[]{:S(2)}) collective-permute-start(f32[136,128]{1,0:T(8,128)S(1)} %add.39), channel_id=1, source_target_pairs={{0,4},{1,5},{2,6},{3,7},{4,0},{5,1},{6,2},{7,3},{8,12},{9,13},{10,... | collective-permute-start | bytes 208904 | tf_op jit(solution)/shard_map/ppermute | solution.py:53
  41.1 2.7 %collective-permute-done.6 = f32[136,128]{1,0:T(8,128)S(1)} collective-permute-done((f32[136,128]{1,0:T(8,128)S(1)}, f32[136,128]{1,0:T(8,128)S(1)}, u32[]{:S(2)}, u32[]{:S(2)}) %collective-permute-start.6) | collective-permute-done | bytes 69664 | tf_op jit(solution)/shard_map/ppermute | solution.py:53
  43.8 2.7 %collective-permute-start.7 = (f32[136,128]{1,0:T(8,128)S(1)}, f32[136,128]{1,0:T(8,128)S(1)}, u32[]{:S(2)}, u32[]{:S(2)}) collective-permute-start(f32[136,128]{1,0:T(8,128)S(1)} %add.40), channel_id=1, source_target_pairs={{0,8},{1,9},{2,10},{3,11},{4,12},{5,13},{6,14},{7,15},{8,0},{9,1},... | collective-permute-start | bytes 208904 | tf_op jit(solution)/shard_map/ppermute | solution.py:53
  46.5 2.6 %collective-permute-done.7 = f32[136,128]{1,0:T(8,128)S(1)} collective-permute-done((f32[136,128]{1,0:T(8,128)S(1)}, f32[136,128]{1,0:T(8,128)S(1)}, u32[]{:S(2)}, u32[]{:S(2)}) %collective-permute-start.7) | collective-permute-done | bytes 69664 | tf_op jit(solution)/shard_map/ppermute | solution.py:53
  49.1 0.9 %collective-permute-start.8 = (f32[136,128]{1,0:T(8,128)S(1)}, f32[136,128]{1,0:T(8,128)S(1)}, u32[]{:S(2)}, u32[]{:S(2)}) collective-permute-start(f32[136,128]{1,0:T(8,128)S(1)} %add.41), channel_id=1, source_target_pairs={{0,16},{1,17},{2,18},{3,19},{4,20},{5,21},{6,22},{7,23},{8,24},{9,... | collective-permute-start | bytes 208904 | tf_op jit(solution)/shard_map/ppermute | solution.py:53
  50.0 3.5 %collective-permute-done.8 = f32[136,128]{1,0:T(8,128)S(1)} collective-permute-done((f32[136,128]{1,0:T(8,128)S(1)}, f32[136,128]{1,0:T(8,128)S(1)}, u32[]{:S(2)}, u32[]{:S(2)}) %collective-permute-start.8) | collective-permute-done | bytes 69664 | tf_op jit(solution)/shard_map/ppermute | solution.py:53
  53.5 0.0 copy-start.1
  53.5 0.1 collective-permute-start.9
  53.6 1.2 %collective-permute-done.9.other_ref = f32[136,128]{1,0:T(8,128)S(1)} collective-permute-done((f32[136,128]{1,0:T(8,128)S(1)}, f32[136,128]{1,0:T(8,128)S(1)}, u32[]{:S(2)}, u32[]{:S(2)}) %collective-permute-start.9) | collective-permute-done | bytes 69664 | tf_op jit(solution)/shard_map/ppermute | solution.py:53
  54.8 0.0 copy-start.5
  54.8 0.0 copy-done.1
  54.8 0.6 copy-done.5
  55.5 12.3 %back.1 = (f32[512,256]{1,0:T(8,128)}, f32[256,256]{1,0:T(8,128)}) custom-call(f32[136,128]{1,0:T(8,128)} %copy-done.1, f32[136,128]{1,0:T(8,128)} %copy-done.5, f32[384,256]{1,0:T(8,128)} %get-tuple-element.10.refs_0_, f32[128,256]{1,0:T(8,128)} %get-tuple-element.11.refs_1_), custom_call_target="tpu_custom_call" | custom-call | tf_op jit(solution)/shard_map/back/pallas_call | solution.py:304
  (5 shorter events, 0.0 us)
Async XLA Ops:
  0.6 4.1 %copy-start = (f32[256,256]{1,0:T(8,128)S(1)}, f32[256,256]{1,0:T(8,128)}, u32[]{:S(2)}) copy-start(f32[256,256]{1,0:T(8,128)} %refs_5_.3) | copy-start | bytes 786436
  1.7 18.5 %collective-permute-start.3 = (f32[256,384]{1,0:T(8,128)S(1)}, f32[256,384]{1,0:T(8,128)S(1)}, u32[]{:S(2)}, u32[]{:S(2)}) collective-permute-start(f32[256,384]{1,0:T(8,128)S(1)} %constant_dynamic-slice_fusion), channel_id=1, source_target_pairs={{0,16},{1,17},{2,18},{3,19},{4,20},{5,21},{6,22},{7,23},{8,24},{9,... | collective-permute-start | bytes 1179656 | tf_op jit(solution)/shard_map/ppermute | solution.py:53
  4.8 11.9 %collective-permute-start.1 = (f32[128,256]{1,0:T(8,128)S(1)}, f32[128,256]{1,0:T(8,128)S(1)}, u32[]{:S(2)}, u32[]{:S(2)}) collective-permute-start(f32[128,256]{1,0:T(8,128)S(1)} %constant_dynamic-slice_fusion.1), channel_id=1, source_target_pairs={{0,16},{1,17},{2,18},{3,19},{4,20},{5,21},{6,22},{7,23},{8,24},{9,... | collective-permute-start | bytes 393224 | tf_op jit(solution)/shard_map/ppermute | solution.py:53
  16.7 1.0 %copy-start.2 = (f32[128,256]{1,0:T(8,128)}, f32[128,256]{1,0:T(8,128)S(1)}, u32[]{:S(2)}) copy-start(f32[128,256]{1,0:T(8,128)S(1)} %collective-permute-done.1.refs_7_) | copy-start | bytes 393220
  16.7 3.5 %collective-permute-start.2 = (f32[128,256]{1,0:T(8,128)S(1)}, f32[128,256]{1,0:T(8,128)S(1)}, u32[]{:S(2)}, u32[]{:S(2)}) collective-permute-start(f32[128,256]{1,0:T(8,128)S(1)} %collective-permute-done.1.refs_7_), channel_id=1, source_target_pairs={{0,1},{1,0},{2,3},{3,2},{4,5},{5,4},{6,7},{7,6},{8,9},{9,8},{10,11... | collective-permute-start | bytes 393224 | tf_op jit(solution)/shard_map/ppermute | solution.py:53
  17.7 1.8 %copy-start.6 = (f32[64]{0:T(128)S(1)}, f32[64]{0:T(128)}, u32[]{:S(2)}) copy-start(f32[64]{0:T(128)} %param.7) | copy-start | bytes 772
  17.7 9.6 %collective-permute-start = (f32[256,128]{1,0:T(8,128)S(1)}, f32[256,128]{1,0:T(8,128)S(1)}, u32[]{:S(2)}, u32[]{:S(2)}) collective-permute-start(f32[256,128]{1,0:T(8,128)S(1)} %constant_dynamic-slice_fusion.2), channel_id=1, source_target_pairs={{0,16},{1,17},{2,18},{3,19},{4,20},{5,21},{6,22},{7,23},{8,24},{9,... | collective-permute-start | bytes 393224 | tf_op jit(solution)/shard_map/ppermute | solution.py:53
  20.2 0.7 copy-start.3
  20.2 0.8 %copy-start.7 = (f32[256,384]{1,0:T(8,128)}, f32[256,384]{1,0:T(8,128)S(1)}, u32[]{:S(2)}) copy-start(f32[256,384]{1,0:T(8,128)S(1)} %collective-permute-done.3.refs_6_) | copy-start | bytes 1179652
  27.3 0.7 copy-start.4
  32.6 1.5 %collective-permute-start.4 = (f32[136,128]{1,0:T(8,128)}, f32[136,128]{1,0:T(8,128)S(1)}, u32[]{:S(2)}, u32[]{:S(2)}) collective-permute-start(f32[136,128]{1,0:T(8,128)} %get-tuple-element.9), channel_id=1, source_target_pairs={{0,1},{1,0},{2,3},{3,2},{4,5},{5,4},{6,7},{7,6},{8,9},{9,8},{10,11... | collective-permute-start | bytes 208904 | tf_op jit(solution)/shard_map/ppermute | solution.py:53
  35.1 4.4 %collective-permute-start.5 = (f32[136,128]{1,0:T(8,128)S(1)}, f32[136,128]{1,0:T(8,128)S(1)}, u32[]{:S(2)}, u32[]{:S(2)}) collective-permute-start(f32[136,128]{1,0:T(8,128)S(1)} %add.38), channel_id=1, source_target_pairs={{0,2},{1,3},{2,0},{3,1},{4,6},{5,7},{6,4},{7,5},{8,10},{9,11},{10,... | collective-permute-start | bytes 208904 | tf_op jit(solution)/shard_map/ppermute | solution.py:53
  39.4 4.4 %collective-permute-start.6 = (f32[136,128]{1,0:T(8,128)S(1)}, f32[136,128]{1,0:T(8,128)S(1)}, u32[]{:S(2)}, u32[]{:S(2)}) collective-permute-start(f32[136,128]{1,0:T(8,128)S(1)} %add.39), channel_id=1, source_target_pairs={{0,4},{1,5},{2,6},{3,7},{4,0},{5,1},{6,2},{7,3},{8,12},{9,13},{10,... | collective-permute-start | bytes 208904 | tf_op jit(solution)/shard_map/ppermute | solution.py:53
  43.8 5.3 %collective-permute-start.7 = (f32[136,128]{1,0:T(8,128)S(1)}, f32[136,128]{1,0:T(8,128)S(1)}, u32[]{:S(2)}, u32[]{:S(2)}) collective-permute-start(f32[136,128]{1,0:T(8,128)S(1)} %add.40), channel_id=1, source_target_pairs={{0,8},{1,9},{2,10},{3,11},{4,12},{5,13},{6,14},{7,15},{8,0},{9,1},... | collective-permute-start | bytes 208904 | tf_op jit(solution)/shard_map/ppermute | solution.py:53
  49.1 4.4 %collective-permute-start.8 = (f32[136,128]{1,0:T(8,128)S(1)}, f32[136,128]{1,0:T(8,128)S(1)}, u32[]{:S(2)}, u32[]{:S(2)}) collective-permute-start(f32[136,128]{1,0:T(8,128)S(1)} %add.41), channel_id=1, source_target_pairs={{0,16},{1,17},{2,18},{3,19},{4,20},{5,21},{6,22},{7,23},{8,24},{9,... | collective-permute-start | bytes 208904 | tf_op jit(solution)/shard_map/ppermute | solution.py:53
  53.5 1.3 %copy-start.1 = (f32[136,128]{1,0:T(8,128)}, f32[136,128]{1,0:T(8,128)S(1)}, u32[]{:S(2)}) copy-start(f32[136,128]{1,0:T(8,128)S(1)} %add.42.part_ref) | copy-start | bytes 208900
  53.5 1.3 %collective-permute-start.9 = (f32[136,128]{1,0:T(8,128)S(1)}, f32[136,128]{1,0:T(8,128)S(1)}, u32[]{:S(2)}, u32[]{:S(2)}) collective-permute-start(f32[136,128]{1,0:T(8,128)S(1)} %add.42.part_ref), channel_id=1, source_target_pairs={{0,1},{1,0},{2,3},{3,2},{4,5},{5,4},{6,7},{7,6},{8,9},{9,8},{10,11... | collective-permute-start | bytes 208904 | tf_op jit(solution)/shard_map/ppermute | solution.py:53
  54.8 0.6 copy-start.5
